TPU v7x, 32 devices: a whole 2x2x4 slice. The times are simulated.
32 devices in a mesh: group: 2 (over core), ctx: 8 (over z, x), mp: 2 (over y).
Axes of the slice: x: 2, y: 2, z: 4, core: 2. Of those that a mesh axis runs over, the one named last changes fastest.
Arguments:
- token_ids: int32 [2, 1024], P('group', 'ctx'), may hold values from 0 to 127
- span_offset: int32 [1], replicated, may hold values from 0 to 3071
- shard_lengths: int32 [8], P('ctx'), may hold values from 1 to 384
- embed_table: bfloat16 [128, 2560], P(None, 'mp'), may hold values from -6 to 6
- norm_gain: bfloat16 [2560], P('mp'), may hold values from 0.25 to 1.75
- query_weight: bfloat16 [2560, 2560], P('mp'), may hold values from -0.25 to 0.25
- key_weight: bfloat16 [2560, 2560], P('mp'), may hold values from -0.25 to 0.25
- value_weight: bfloat16 [2560, 2560], P('mp'), may hold values from -0.125 to 0.125
- cache_keys: bfloat16 [3072, 2560], P('ctx', 'mp'), may hold values from -440 to 440
- cache_values: bfloat16 [3072, 2560], P('ctx', 'mp'), may hold values from -6 to 6
Outputs:
- attended: bfloat16 [2, 1024, 2560], P('group', 'ctx', 'mp')
All inputs are finite; a program needn't handle non-finite values.
Results may differ from a plain program's by a relative error of at most 0.012.
The roundings to bfloat16 on the way count: a program that leaves them out, or rounds other values in their place, can miss the bound.
Values may be sent and summed in bfloat16 or wider, within the bound.
A program may use at most 256 MiB of HBM per device.

v0:
```python
import math
import jax
import jax.numpy as jnp
from jax import lax
from jax.sharding import PartitionSpec as P

D = 2560
HD = 80
PROT = 256
STEPS = 4


def passed_along(value, axis, steps):
    count = lax.axis_size(axis)
    first, last = (max(0, -steps), min(count, count - steps))
    return lax.ppermute(value, axis, [(source, source + steps) for source in range(first, last)])


def rotate(values_in, positions):
    row_count = values_in.shape[0]
    head_count = values_in.shape[1] // HD
    quarter = HD // 4
    column = (positions % PROT).astype(jnp.float32)
    homolog = (positions // PROT).astype(jnp.float32)
    frequency = 10000.0 ** (-jnp.arange(quarter, dtype=jnp.float32) / quarter)
    angles = jnp.stack([column[:, None] * frequency, homolog[:, None] * frequency], 1)
    cosine = jnp.cos(angles)[:, None, :, None, :]
    sine_table = jnp.sin(angles)[:, None, :, None, :]
    pieces = values_in.reshape(row_count, head_count, 2, 2, quarter)
    partner = jnp.stack([-pieces[:, :, :, 1], pieces[:, :, :, 0]], 3)
    return (pieces * cosine + partner * sine_table).reshape(row_count, head_count * HD)


def block_partial(
    query_block, start, all_keys, all_values, live_length, span_base, cache_count, decoding
):
    block_rows = query_block.shape[0]
    head_count = query_block.shape[1] // HD
    key_slots = all_keys.shape[0]
    query_heads = query_block.reshape(block_rows, head_count, HD)
    key_heads = all_keys.reshape(key_slots, head_count, HD)
    value_heads = all_values.reshape(key_slots, head_count, HD)
    scores = jnp.einsum(
        "qhd,khd->hqk", query_heads, key_heads, preferred_element_type=jnp.float32
    ) * (1.0 / math.sqrt(HD))
    slot = jnp.arange(key_slots, dtype=jnp.int32)
    query_index = start + jnp.arange(block_rows, dtype=jnp.int32)
    cache_live = (slot < cache_count) & (slot < live_length)
    span_index = span_base + slot - cache_count
    span_seen = (slot >= cache_count)[None, :] & (
        decoding | (span_index[None, :] <= query_index[:, None])
    )
    visible = (cache_live[None, :] | span_seen)[None]
    block_max = jnp.max(jnp.where(visible, scores, -1e30), -1)
    weights = jnp.where(visible, jnp.exp(scores - block_max[..., None]), 0.0)
    block_sum = jnp.sum(weights, -1)
    block_acc = jnp.einsum(
        "hqk,khd->qhd",
        weights.astype(jnp.bfloat16),
        value_heads,
        preferred_element_type=jnp.float32,
    )
    return (block_max.T, block_sum.T, block_acc.reshape(block_rows, head_count * HD))


def local(
    token_ids,
    span_offset,
    shard_lengths,
    embed_table,
    norm_gain,
    query_weight,
    key_weight,
    value_weight,
    cache_keys,
    cache_values,
):
    token_row = token_ids[0]
    row_count = token_row.shape[0]
    ctx_count = lax.axis_size("ctx")
    ctx_index = lax.axis_index("ctx")
    decoding = lax.axis_index("group") == 1
    one_hot = (
        token_row[:, None] == jnp.arange(embed_table.shape[0], dtype=jnp.int32)[None, :]
    ).astype(jnp.bfloat16)
    embedded = jnp.dot(one_hot, embed_table, preferred_element_type=jnp.float32)
    square_sum = lax.psum(jnp.sum(embedded * embedded, 1), "mp")
    normal_rows = (
        embedded * lax.rsqrt(square_sum / D + 1e-05)[:, None] * norm_gain.astype(jnp.float32)
    ).astype(jnp.bfloat16)
    query_part = jnp.dot(normal_rows, query_weight, preferred_element_type=jnp.float32)
    key_part = jnp.dot(normal_rows, key_weight, preferred_element_type=jnp.float32)
    value_part = jnp.dot(normal_rows, value_weight, preferred_element_type=jnp.float32)
    query_full, key_full, value_full = (
        lax.psum_scatter(query_part, "mp", scatter_dimension=1, tiled=True),
        lax.psum_scatter(key_part, "mp", scatter_dimension=1, tiled=True),
        lax.psum_scatter(value_part, "mp", scatter_dimension=1, tiled=True),
    )
    offset_value = span_offset[0]
    local_iota = jnp.arange(row_count, dtype=jnp.int32)
    positions = jnp.where(
        decoding,
        offset_value + row_count * ctx_count + local_iota % STEPS,
        offset_value + ctx_index * row_count + local_iota,
    )
    queries = rotate(query_full, positions).astype(jnp.bfloat16)
    new_keys = rotate(key_full, positions).astype(jnp.bfloat16)
    new_values = value_full.astype(jnp.bfloat16)
    width = queries.shape[1]
    head_count = width // HD
    span_keys, span_values = passed_along((new_keys, new_values), "group", 1)
    block_keys = jnp.where(decoding, span_keys, new_keys)
    block_values = jnp.where(decoding, span_values, new_values)
    cache_count = cache_keys.shape[0]
    all_keys = jnp.concatenate([cache_keys, block_keys], 0)
    all_values = jnp.concatenate([cache_values, block_values], 0)
    live_length = shard_lengths[0]
    span_base = ctx_index * row_count
    gathered = lax.all_gather(queries, "ctx", axis=0, tiled=True)
    total = gathered.shape[0]
    block_rows = math.gcd(total, 512)
    block_count = total // block_rows
    block_starts = jnp.arange(block_count, dtype=jnp.int32) * block_rows

    def one_block(pair):
        return block_partial(
            pair[0], pair[1], all_keys, all_values, live_length, span_base, cache_count, decoding
        )

    maxima, totals, sums = lax.map(
        one_block, (gathered.reshape(block_count, block_rows, width), block_starts)
    )
    maxima = maxima.reshape(total, head_count)
    totals = totals.reshape(total, head_count)
    sums = sums.reshape(total, width)
    got_max, got_sum, got_acc = (
        lax.all_to_all(maxima[None], "ctx", split_axis=1, concat_axis=0, tiled=True),
        lax.all_to_all(totals[None], "ctx", split_axis=1, concat_axis=0, tiled=True),
        lax.all_to_all(sums[None], "ctx", split_axis=1, concat_axis=0, tiled=True),
    )
    whole_max = jnp.max(got_max, 0)
    rescale = jnp.exp(got_max - whole_max[None])
    whole_sum = jnp.sum(rescale * got_sum, 0)
    whole_acc = jnp.sum(got_acc * jnp.repeat(rescale, HD, axis=2), 0)
    cands = row_count // STEPS
    own_q = queries.reshape(cands, STEPS, head_count, HD)
    own_k = new_keys.reshape(cands, STEPS, head_count, HD)
    own_v = new_values.reshape(cands, STEPS, head_count, HD)
    own_scores = jnp.einsum("ashd,athd->ahst", own_q, own_k, preferred_element_type=jnp.float32) * (
        1.0 / math.sqrt(HD)
    )
    step_iota = jnp.arange(STEPS, dtype=jnp.int32)
    own_visible = (step_iota[None, :] <= step_iota[:, None]) & decoding
    own_max = jnp.max(jnp.where(own_visible, own_scores, -1e30), -1)
    final_max = jnp.maximum(whole_max, own_max.transpose(0, 2, 1).reshape(row_count, head_count))
    keep_old = jnp.exp(whole_max - final_max)
    final_cand = final_max.reshape(cands, STEPS, head_count).transpose(0, 2, 1)
    own_weights = jnp.where(own_visible, jnp.exp(own_scores - final_cand[..., None]), 0.0)
    own_sum = jnp.sum(own_weights, -1).transpose(0, 2, 1).reshape(row_count, head_count)
    own_acc = jnp.einsum(
        "ahst,athd->ashd",
        own_weights.astype(jnp.bfloat16),
        own_v,
        preferred_element_type=jnp.float32,
    ).reshape(row_count, width)
    numer = whole_acc * jnp.repeat(keep_old, HD, axis=1) + own_acc
    denom = whole_sum * keep_old + own_sum
    output = numer / jnp.repeat(denom, HD, axis=1)
    return output.astype(jnp.bfloat16)[None]


def solution(mesh):
    placed = (
        P("group", "ctx"),
        P(),
        P("ctx"),
        P(None, "mp"),
        P("mp"),
        P("mp", None),
        P("mp", None),
        P("mp", None),
        P("ctx", "mp"),
        P("ctx", "mp"),
    )
    return jax.shard_map(
        local, mesh=mesh, in_specs=placed, out_specs=P("group", "ctx", "mp"), check_vma=False
    )
```

profile of v0, /device:TPU:0, one launch (start us, length us, event | category | flops | bytes accessed | tf_op | source)
XLA Modules:
  0.0 382.4 jit_solution(8588172545605878299)
XLA Ops:
  8.5 5.9 %psum.7 = f32[128]{0:T(128)S(1)} all-reduce(f32[128]{0:T(128)S(1)} %get-tuple-element.257), channel_id=1, replica_groups=mesh['group'=2,'ctx'=8,'mp'=2] {'mp'}, use_global_device_ids=true, to_apply=%region_1.0 | all-reduce | flops 128 | bytes 1024 | tf_op jit(solution)/shard_map/psum | solution.py:87
  14.6 5.0 %fusion.29 = f32[128,2560]{1,0:T(8,128)} fusion(bf16[128,1280]{1,0:T(8,128)(2,1)S(1)} %multiply_convert_fusion, bf16[1280,2560]{1,0:T(8,128)(2,1)} %param.18), kind=kOutput, calls=%fused_computation.76 | convolution fusion | flops 838860800 | bytes 8192000 | tf_op jit(solution)/shard_map/dot_general | solution.py:92
  19.6 5.0 %fusion.28 = f32[128,2560]{1,0:T(8,128)} fusion(bf16[128,1280]{1,0:T(8,128)(2,1)S(1)} %multiply_convert_fusion, bf16[1280,2560]{1,0:T(8,128)(2,1)} %param.17), kind=kOutput, calls=%fused_computation.75 | convolution fusion | flops 838860800 | bytes 8192000 | tf_op jit(solution)/shard_map/dot_general | solution.py:91
  24.7 5.0 %fusion.30 = f32[128,2560]{1,0:T(8,128)} fusion(bf16[128,1280]{1,0:T(8,128)(2,1)S(1)} %multiply_convert_fusion, bf16[1280,2560]{1,0:T(8,128)(2,1)} %param.19), kind=kOutput, calls=%fused_computation.77 | convolution fusion | flops 838860800 | bytes 8192000 | tf_op jit(solution)/shard_map/dot_general | solution.py:93
  31.9 12.9 %reduce-scatter.6.cloned.1.call-done = f32[128,1280]{1,0:T(8,128)} async-done(((f32[128,2560]{1,0:T(8,128)}), f32[128,1280]{1,0:T(8,128)}) %reduce-scatter.6.cloned.1.call-update) | async-done | bytes 655376 | tf_op jit(solution)/shard_map/reduce_scatter | solution.py:96
  46.2 24.2 %reduce-scatter.4.cloned.1.call-done = f32[128,1280]{1,0:T(8,128)} async-done(((f32[128,2560]{1,0:T(8,128)}), f32[128,1280]{1,0:T(8,128)}) %reduce-scatter.4.cloned.1.call-update) | async-done | bytes 655376 | tf_op jit(solution)/shard_map/reduce_scatter | solution.py:95
  73.4 2.6 add_convert_fusion.1
  81.0 14.9 %reduce-scatter.8.cloned.1.call-done = f32[128,1280]{1,0:T(8,128)} async-done(((f32[128,2560]{1,0:T(8,128)}), f32[128,1280]{1,0:T(8,128)}) %reduce-scatter.8.cloned.1.call-update) | async-done | bytes 655376 | tf_op jit(solution)/shard_map/reduce_scatter | solution.py:97
  97.0 2.3 collective-permute-start.1
  100.0 1.9 broadcast_select_fusion
  105.4 46.9 %all-gather.2.cloned.1.call-done = bf16[1024,1280]{1,0:T(8,128)(2,1)} async-done(((bf16[128,1280]{1,0:T(8,128)(2,1)}), bf16[1024,1280]{1,0:T(8,128)(2,1)}) %all-gather.2.cloned.1.call-update) | async-done | bytes 2621456 | tf_op jit(solution)/shard_map/all_gather | solution.py:119
  152.3 70.8 %while.16 = (s32[]{:T(128)}, f32[2,512,16]{1,2,0:T(8,128)S(1)}, f32[2,512,16]{1,2,0:T(8,128)S(1)}, f32[2,512,1280]{2,1,0:T(8,128)}, s32[]{:T(128)}, /*index=5*/p...) while((s32[]{:T(128)}, f32[2,512,16]{1,2,0:T(8,128)S(1)}, ...), condition=%wide.region_8.9_spmd, body=%wide.region_5.8_spmd.sunk | while | flops 1389350400 | bytes 79177912 | solution.py:130
  156.7 8.8 %select_reduce_fusion.3 = (f32[16,512]{1,0:T(8,128)S(1)}, f32[16,512,512]{1,2,0:T(8,128)}) fusion(pred[512,512]{0,1:T(8,128)(4,1)S(1)} %and_or_fusion.2, bf16[512,16,80]{0,2,1:T(8,128)(2,1)S(1)} %bitcast.97, bf16[512,16,80]{0,2,1:T(8,128)(2,1)} %bitcast.99), kind=kOutput, calls=%fused_computation.1.clone.1 | convolution fusion | flops 683663360 | bytes 19693568 | tf_op jit(solution)/shard_map/while/body/eval_jaxpr/qhd,khd->hqk/dot_general | solution.py:43
  165.5 9.3 %fusion.54 = f32[16,512]{1,0:T(8,128)S(1)} fusion(f32[16,512,512]{1,2,0:T(8,128)} %get-tuple-element.334, f32[16,512]{1,0:T(8,128)S(1)} %get-tuple-element.335, pred[512,512]{0,1:T(8,128)(4,1)S(1)} %and_or_fusion.2), kind=kLoop, calls=%fused_computation.3.clone.1 | loop fusion | flops 16769024 | bytes 17104896 | tf_op jit(solution)/shard_map/while/body/eval_jaxpr/reduce_sum | solution.py:56
  174.7 9.2 %fusion.55 = f32[16,512,80]{1,2,0:T(8,128)} fusion(bf16[512,16,80]{0,2,1:T(8,128)(2,1)S(1)} %bitcast.111, f32[16,512,512]{1,2,0:T(8,128)} %get-tuple-element.334, f32[16,512]{1,0:T(8,128)S(1)} %get-tuple-element.335, pred[512,512]{0,1:T(8,128)(4,1)S(1)} %and_or_fusion.2), kind=kOutput, calls=%fused_computation.4.clone.1 | convolution fusion | flops 687865856 | bytes 21004288 | tf_op jit(solution)/shard_map/while/body/eval_jaxpr/hqk,khd->qhd/dot_general | solution.py:57
  183.9 2.1 copy.222
  192.1 8.8 %select_reduce_fusion.3 = (f32[16,512]{1,0:T(8,128)S(1)}, f32[16,512,512]{1,2,0:T(8,128)}) fusion(pred[512,512]{0,1:T(8,128)(4,1)S(1)} %and_or_fusion.2, bf16[512,16,80]{0,2,1:T(8,128)(2,1)S(1)} %bitcast.97, bf16[512,16,80]{0,2,1:T(8,128)(2,1)} %bitcast.99), kind=kOutput, calls=%fused_computation.1.clone.1 | convolution fusion | flops 683663360 | bytes 19693568 | tf_op jit(solution)/shard_map/while/body/eval_jaxpr/qhd,khd->hqk/dot_general | solution.py:43
  200.8 9.3 %fusion.54 = f32[16,512]{1,0:T(8,128)S(1)} fusion(f32[16,512,512]{1,2,0:T(8,128)} %get-tuple-element.334, f32[16,512]{1,0:T(8,128)S(1)} %get-tuple-element.335, pred[512,512]{0,1:T(8,128)(4,1)S(1)} %and_or_fusion.2), kind=kLoop, calls=%fused_computation.3.clone.1 | loop fusion | flops 16769024 | bytes 17104896 | tf_op jit(solution)/shard_map/while/body/eval_jaxpr/reduce_sum | solution.py:56
  210.1 9.2 %fusion.55 = f32[16,512,80]{1,2,0:T(8,128)} fusion(bf16[512,16,80]{0,2,1:T(8,128)(2,1)S(1)} %bitcast.111, f32[16,512,512]{1,2,0:T(8,128)} %get-tuple-element.334, f32[16,512]{1,0:T(8,128)S(1)} %get-tuple-element.335, pred[512,512]{0,1:T(8,128)(4,1)S(1)} %and_or_fusion.2), kind=kOutput, calls=%fused_computation.4.clone.1 | convolution fusion | flops 687865856 | bytes 21004288 | tf_op jit(solution)/shard_map/while/body/eval_jaxpr/hqk,khd->qhd/dot_general | solution.py:57
  219.3 2.1 copy.222
  221.4 1.7 constant_dynamic-update-slice_fusion.2
  223.9 2.0 reduce
  226.7 3.6 all-to-all-start.1
  230.5 2.0 reduce.2
  233.4 3.6 all-to-all-done.1
  236.9 3.3 all-to-all-start.2
  240.3 10.2 %copy.168 = f32[1,1024,1280]{2,0,1:T(1,128)} copy(f32[1,1024,1280]{2,1,0:T(8,128)} %bitcast.103) | data formatting | bytes 10485760 | tf_op jit(solution)/shard_map/broadcast_in_dim;reshape | solution.py:139
  250.5 6.1 %all-to-all-start = ((f32[1,1024,1280]{2,0,1:T(1,128)}), f32[1,1024,1280]{2,0,1:T(1,128)}, u32[]{:S(2)}, u32[]{:S(2)}) async-start(f32[1,1024,1280]{2,0,1:T(1,128)} %copy.168), calls=%async_computation.3 | async-start | bytes 10485760 | tf_op jit(solution)/shard_map/all_to_all | solution.py:139
  268.6 2.6 broadcast_in_dim.99
  271.2 5.9 %copy.174 = f32[8,128,1280]{2,1,0:T(8,128)} copy(f32[8,128,1280]{1,2,0:T(8,128)} %bitcast.101) | data formatting | bytes 10485760 | tf_op jit(solution)/shard_map/reshape | solution.py:144
  277.1 92.9 %all-to-all-done = f32[1,1024,1280]{2,0,1:T(1,128)} async-done(((f32[1,1024,1280]{2,0,1:T(1,128)}), f32[1,1024,1280]{2,0,1:T(1,128)}, u32[]{:S(2)}, u32[]{:S(2)}) %all-to-all-start) | async-done | bytes 5242912 | tf_op jit(solution)/shard_map/all_to_all | solution.py:139
  370.0 3.0 copy.203
  (122 shorter events, 46.0 us)
Async XLA Ops:
  6.5 1.0 copy-start
  6.5 38.2 %reduce-scatter.6.cloned.1.call-start = ((), (), s32[]{:S(2)}) async-start(), calls=%async_computation.8 | async-start | bytes 1966080 | tf_op jit(solution)/shard_map/reduce_scatter | solution.py:96
  19.6 50.7 %reduce-scatter.4.cloned.1.call-start = ((), (), s32[]{:S(2)}) async-start(), calls=%async_computation.6 | async-start | bytes 1966080 | tf_op jit(solution)/shard_map/reduce_scatter | solution.py:95
  24.6 71.3 %reduce-scatter.8.cloned.1.call-start = ((), (), s32[]{:S(2)}) async-start(), calls=%async_computation.9 | async-start | bytes 1966080 | tf_op jit(solution)/shard_map/reduce_scatter | solution.py:97
  29.7 122.6 %all-gather.2.cloned.1.call-start = ((), (), s32[]{:S(2)}) async-start(), calls=%async_computation.7 | async-start | bytes 2949120 | tf_op jit(solution)/shard_map/all_gather | solution.py:119
  76.0 23.3 %collective-permute-start = (bf16[128,1280]{1,0:T(8,128)(2,1)S(1)}, bf16[128,1280]{1,0:T(8,128)(2,1)S(1)}, u32[]{:S(2)}, u32[]{:S(2)}) collective-permute-start(bf16[128,1280]{1,0:T(8,128)(2,1)S(1)} %get-tuple-element.248), channel_id=1, source_target_pairs={{0,16},{1,17},{2,18},{3,19},{4,20},{5,21},{6,22},{7,23},{8,24},{9,... | collective-permute-start | bytes 983048 | tf_op jit(solution)/shard_map/ppermute | solution.py:16
  97.0 55.3 %copy-start.5 = (bf16[128,1280]{1,0:T(8,128)(2,1)}, bf16[128,1280]{1,0:T(8,128)(2,1)S(1)}, u32[]{:S(2)}) copy-start(bf16[128,1280]{1,0:T(8,128)(2,1)S(1)} %convert_element_type.57) | copy-start | bytes 983044
  97.0 2.9 collective-permute-start.1
  165.5 9.3 %copy-start.4 = (bf16[512,1280]{0,1:T(8,128)(2,1)S(1)}, bf16[512,1280]{0,1:T(8,128)(2,1)}, u32[]{:S(2)}) copy-start(bf16[512,1280]{0,1:T(8,128)(2,1)} %get-tuple-element.372) | copy-start | bytes 3932164 | tf_op jit(solution)/shard_map/while
  200.8 9.3 %copy-start.4 = (bf16[512,1280]{0,1:T(8,128)(2,1)S(1)}, bf16[512,1280]{0,1:T(8,128)(2,1)}, u32[]{:S(2)}) copy-start(bf16[512,1280]{0,1:T(8,128)(2,1)} %get-tuple-element.372) | copy-start | bytes 3932164 | tf_op jit(solution)/shard_map/while
  226.7 10.2 %all-to-all-start.1 = ((f32[8,1,2048]{2,1,0:T(1,128)}), f32[8,1,2048]{2,1,0:T(1,128)S(1)}, u32[]{:S(2)}, u32[]{:S(2)}) async-start(f32[8,1,2048]{2,1,0:T(1,128)} %reshape.390), calls=%async_computation.4 | async-start | bytes 131072 | tf_op jit(solution)/shard_map/all_to_all | solution.py:137
  236.9 13.6 %all-to-all-start.2 = ((f32[8,1,2048]{2,1,0:T(1,128)}), f32[8,1,2048]{2,1,0:T(1,128)S(1)}, u32[]{:S(2)}, u32[]{:S(2)}) async-start(f32[8,1,2048]{2,1,0:T(1,128)} %reshape.392), calls=%async_computation.5 | async-start | bytes 131072 | tf_op jit(solution)/shard_map/all_to_all | solution.py:138
  250.5 6.9 %copy-start.3 = (bf16[128,1280]{1,0:T(8,128)(2,1)S(1)}, bf16[128,1280]{1,0:T(8,128)(2,1)}, u32[]{:S(2)}) copy-start(bf16[128,1280]{1,0:T(8,128)(2,1)} %get-tuple-element.247) | copy-start | bytes 983044
  250.5 7.7 %copy-start.6 = (bf16[128,1280]{1,0:T(8,128)(2,1)S(1)}, bf16[128,1280]{1,0:T(8,128)(2,1)}, u32[]{:S(2)}) copy-start(bf16[128,1280]{1,0:T(8,128)(2,1)} %copy-done.5) | copy-start | bytes 983044
  250.5 119.5 %all-to-all-start = ((f32[1,1024,1280]{2,0,1:T(1,128)}), f32[1,1024,1280]{2,0,1:T(1,128)}, u32[]{:S(2)}, u32[]{:S(2)}) async-start(f32[1,1024,1280]{2,0,1:T(1,128)} %copy.168), calls=%async_computation.3 | async-start | bytes 10485760 | tf_op jit(solution)/shard_map/all_to_all | solution.py:139
  370.0 4.0 %copy-start.2 = (f32[8,128,1280]{2,1,0:T(8,128)S(1)}, f32[8,128,1280]{2,1,0:T(8,128)}, u32[]{:S(2)}) copy-start(f32[8,128,1280]{2,1,0:T(8,128)} %copy.174) | copy-start | bytes 15728644
  373.0 2.9 copy-start.1
Sparse Core Ops, SparseCore 0:
  19.7 25.0 reduce-scatter.5
  47.0 23.2 reduce-scatter.3
  72.6 23.2 reduce-scatter.7
  97.9 54.3 all-gather.1
where the time goes:
time: 384 us; the launch traced here: 382 us
  waiting for transfers between devices  196 us (51%)
  local copies, waits for them, and re-layouts  57.1 us (15%)
  matrix products  53.2 us (14%)
  other arithmetic  38.9 us (10%)
  starting transfers between devices  17 us (4%)
  between operations  14.2 us (4%)
  blocking collectives  5.9 us (2%)
    all_to_all x1, waiting for transfers between devices, local(): lax.all_to_all(sums[None], 'ctx', split_axis=1, concat_axis=0, tiled=True)  92.9 us
    all_gather x1, waiting for transfers between devices, local(): gathered = lax.all_gather(queries, 'ctx', axis=0, tiled=True)  46.9 us
    reduce_scatter x1, waiting for transfers between devices, local(): lax.psum_scatter(query_part, 'mp', scatter_dimension=1, tiled=True)  24.2 us
    reduce_sum x2, other arithmetic, block_partial(): block_sum = jnp.sum(weights, -1)  18.5 us
    dot_general x2, matrix products, block_partial(): jnp.einsum('hqk,khd->qhd', weights.astype(jnp.bfloat16), value_heads, pre...  18.3 us
    dot_general x2, matrix products, block_partial(): jnp.einsum('qhd,khd->hqk', query_heads, key_heads, preferred_element_type...  17.6 us
    reduce_scatter x1, waiting for transfers between devices, local(): lax.psum_scatter(value_part, 'mp', scatter_dimension=1, tiled=True)  14.9 us
    reduce_scatter x1, waiting for transfers between devices, local(): lax.psum_scatter(key_part, 'mp', scatter_dimension=1, tiled=True)  12.9 us
  transfers between devices with their start and end apart: 9, of which 7 were waited for; matrix products, arithmetic and copies ran while one was open for 16% of the time, Pallas kernels for 0%

commit v1 on v0

--- a/solution.py
+++ b/solution.py
@@ -1,3 +1,4 @@
+import functools
 import math
 import jax
 import jax.numpy as jnp
@@ -8,6 +9,22 @@
 HD = 80
 PROT = 256
 STEPS = 4
+
+
+def return_all_surface(chunk, comm_axis):
+    num_devices = lax.psum(1, comm_axis)
+    rack = tuple(((dev_j, (dev_j + 1) % num_devices) for dev_j in range(num_devices)))
+    z1 = [None] * num_devices
+    z1[num_devices - 1] = chunk
+    for j0 in range(num_devices - 2, -1, -1):
+        z1[j0] = lax.ppermute(z1[j0 + 1], comm_axis, perm=rack)
+    tile_out = jnp.concatenate(z1, axis=0)
+    block_next = lax.axis_index(comm_axis)
+    y_new = (block_next + 1) * chunk.shape[0]
+    return jnp.roll(tile_out, y_new, 0)
+
+
+_guide_record = functools.partial(return_all_surface, comm_axis="ctx")
 
 
 def passed_along(value, axis, steps):
@@ -116,7 +133,7 @@
     all_values = jnp.concatenate([cache_values, block_values], 0)
     live_length = shard_lengths[0]
     span_base = ctx_index * row_count
-    gathered = lax.all_gather(queries, "ctx", axis=0, tiled=True)
+    gathered = _guide_record(queries)
     total = gathered.shape[0]
     block_rows = math.gcd(total, 512)
     block_count = total // block_rows

time: 384 us -> 391 us (1.018); the launches traced: 382 us -> 384 us
  waiting for transfers between devices: 196 us -> 182 us
  local copies, waits for them, and re-layouts: 57.1 us -> 68.8 us
    ppermute x0 -> x7, waiting for transfers between devices: none -> 57.3 us  [return_all_surface(): z1[j0] = lax.ppermute(z1[j0 + 1], comm_axis, perm=rack)]
    all_gather x1 -> x0, waiting for transfers between devices: 46.9 us -> none  [local(): gathered = lax.all_gather(queries, 'ctx', axis=0, tiled=True)]
    reduce_scatter x1, waiting for transfers between devices: 14.9 us -> 0.02 us  [local(): lax.psum_scatter(value_part, 'mp', scatter_dimension=1, tiled=True)]
    all_to_all x1, waiting for transfers between devices: 92.9 us -> 83.8 us  [local(): lax.all_to_all(sums[None], 'ctx', split_axis=1, concat_axis=0, tiled=True)]
    unnamed x22 -> x47, local copies, waits for them, and re-layouts: 11.9 us -> 20 us
  transfers between devices with their start and end apart: 9 -> 15, of which waited for: 7 -> 11; matrix products, arithmetic and copies ran while one was open for 16% -> 17% of each run, Pallas kernels for 0% -> 0%
where the time goes in v1:
time: 391 us; the launch traced here: 384 us
  waiting for transfers between devices  182 us (47%)
  local copies, waits for them, and re-layouts  68.8 us (18%)
  matrix products  54.2 us (14%)
  other arithmetic  39.1 us (10%)
  starting transfers between devices  19.3 us (5%)
  between operations  14.6 us (4%)
  blocking collectives  5.9 us (2%)
    all_to_all x1, waiting for transfers between devices, local(): lax.all_to_all(sums[None], 'ctx', split_axis=1, concat_axis=0, tiled=True)  83.8 us
    ppermute x7, waiting for transfers between devices, return_all_surface(): z1[j0] = lax.ppermute(z1[j0 + 1], comm_axis, perm=rack)  57.3 us
    reduce_scatter x1, waiting for transfers between devices, local(): lax.psum_scatter(query_part, 'mp', scatter_dimension=1, tiled=True)  24.2 us
    unnamed x47, local copies, waits for them, and re-layouts  20 us
    reduce_sum x2, other arithmetic, block_partial(): block_sum = jnp.sum(weights, -1)  18.5 us
    dot_general x2, matrix products, block_partial(): jnp.einsum('hqk,khd->qhd', weights.astype(jnp.bfloat16), value_heads, pre...  18.3 us
    dot_general x2, matrix products, block_partial(): jnp.einsum('qhd,khd->hqk', query_heads, key_heads, preferred_element_type...  17.6 us
    reduce_scatter x1, waiting for transfers between devices, local(): lax.psum_scatter(key_part, 'mp', scatter_dimension=1, tiled=True)  13 us
  transfers between devices with their start and end apart: 15, of which 11 were waited for; matrix products, arithmetic and copies ran while one was open for 17% of the time, Pallas kernels for 0%

profile of v1, /device:TPU:0, one launch (start us, length us, event | category | flops | bytes accessed | tf_op | source)
XLA Modules:
  0.0 384.2 jit_solution(4868836382360753540)
XLA Ops:
  8.5 5.9 %psum.7 = f32[128]{0:T(128)S(1)} all-reduce(f32[128]{0:T(128)S(1)} %get-tuple-element.246), channel_id=1, replica_groups=mesh['group'=2,'ctx'=8,'mp'=2] {'mp'}, use_global_device_ids=true, to_apply=%region_1.0 | all-reduce | flops 128 | bytes 1024 | tf_op jit(solution)/shard_map/psum | solution.py:104
  14.6 5.0 %fusion.29 = f32[128,2560]{1,0:T(8,128)} fusion(bf16[128,1280]{1,0:T(8,128)(2,1)S(1)} %multiply_convert_fusion, bf16[1280,2560]{1,0:T(8,128)(2,1)} %param.18), kind=kOutput, calls=%fused_computation.93 | convolution fusion | flops 838860800 | bytes 8192000 | tf_op jit(solution)/shard_map/dot_general | solution.py:109
  19.6 5.0 %fusion.28 = f32[128,2560]{1,0:T(8,128)} fusion(bf16[128,1280]{1,0:T(8,128)(2,1)S(1)} %multiply_convert_fusion, bf16[1280,2560]{1,0:T(8,128)(2,1)} %param.17), kind=kOutput, calls=%fused_computation.92 | convolution fusion | flops 838860800 | bytes 8192000 | tf_op jit(solution)/shard_map/dot_general | solution.py:108
  24.7 5.0 %fusion.30 = f32[128,2560]{1,0:T(8,128)} fusion(bf16[128,1280]{1,0:T(8,128)(2,1)S(1)} %multiply_convert_fusion, bf16[1280,2560]{1,0:T(8,128)(2,1)} %param.19), kind=kOutput, calls=%fused_computation.94 | convolution fusion | flops 838860800 | bytes 8192000 | tf_op jit(solution)/shard_map/dot_general | solution.py:110
  31.8 13.0 %reduce-scatter.6.cloned.1.call-done = f32[128,1280]{1,0:T(8,128)} async-done(((f32[128,2560]{1,0:T(8,128)}), f32[128,1280]{1,0:T(8,128)}) %reduce-scatter.6.cloned.1.call-update) | async-done | bytes 655376 | tf_op jit(solution)/shard_map/reduce_scatter | solution.py:113
  46.2 24.2 %reduce-scatter.4.cloned.1.call-done = f32[128,1280]{1,0:T(8,128)} async-done(((f32[128,2560]{1,0:T(8,128)}), f32[128,1280]{1,0:T(8,128)}) %reduce-scatter.4.cloned.1.call-update) | async-done | bytes 655376 | tf_op jit(solution)/shard_map/reduce_scatter | solution.py:112
  76.9 10.5 %collective-permute-done = bf16[128,1280]{1,0:T(8,128)(2,1)S(1)} collective-permute-done((bf16[128,1280]{1,0:T(8,128)(2,1)S(1)}, bf16[128,1280]{1,0:T(8,128)(2,1)S(1)}, u32[]{:S(2)}, u32[]{:S(2)}) %collective-permute-start) | collective-permute-done | bytes 327712 | tf_op jit(solution)/shard_map/ppermute | solution.py:20
  87.4 11.1 %collective-permute-done.1 = bf16[128,1280]{1,0:T(8,128)(2,1)S(1)} collective-permute-done((bf16[128,1280]{1,0:T(8,128)(2,1)S(1)}, bf16[128,1280]{1,0:T(8,128)(2,1)S(1)}, u32[]{:S(2)}, u32[]{:S(2)}) %collective-permute-start.1) | collective-permute-done | bytes 327712 | tf_op jit(solution)/shard_map/ppermute | solution.py:20
  98.5 10.3 %collective-permute-done.2 = bf16[128,1280]{1,0:T(8,128)(2,1)S(1)} collective-permute-done((bf16[128,1280]{1,0:T(8,128)(2,1)S(1)}, bf16[128,1280]{1,0:T(8,128)(2,1)S(1)}, u32[]{:S(2)}, u32[]{:S(2)}) %collective-permute-start.2) | collective-permute-done | bytes 327712 | tf_op jit(solution)/shard_map/ppermute | solution.py:20
  108.8 2.0 collective-permute-start.7
  115.9 2.0 collective-permute-start.8
  118.9 9.8 %collective-permute-done.4 = bf16[128,1280]{1,0:T(8,128)(2,1)} collective-permute-done((bf16[128,1280]{1,0:T(8,128)(2,1)}, bf16[128,1280]{1,0:T(8,128)(2,1)}, u32[]{:S(2)}, u32[]{:S(2)}) %collective-permute-start.4) | collective-permute-done | bytes 327712 | tf_op jit(solution)/shard_map/ppermute | solution.py:20
  130.6 8.5 %collective-permute-done.5 = bf16[128,1280]{1,0:T(8,128)(2,1)} collective-permute-done((bf16[128,1280]{1,0:T(8,128)(2,1)}, bf16[128,1280]{1,0:T(8,128)(2,1)}, u32[]{:S(2)}, u32[]{:S(2)}) %collective-permute-start.5) | collective-permute-done | bytes 327712 | tf_op jit(solution)/shard_map/ppermute | solution.py:20
  143.3 6.4 %collective-permute-done.6 = bf16[128,1280]{1,0:T(8,128)(2,1)} collective-permute-done((bf16[128,1280]{1,0:T(8,128)(2,1)}, bf16[128,1280]{1,0:T(8,128)(2,1)}, u32[]{:S(2)}, u32[]{:S(2)}) %collective-permute-start.6) | collective-permute-done | bytes 327712 | tf_op jit(solution)/shard_map/ppermute | solution.py:20
  159.6 71.0 %while.16 = (s32[]{:T(128)}, f32[2,512,16]{1,2,0:T(8,128)S(1)}, f32[2,512,16]{1,2,0:T(8,128)S(1)}, f32[2,512,1280]{2,1,0:T(8,128)}, s32[]{:T(128)}, /*index=5*/p...) while((s32[]{:T(128)}, f32[2,512,16]{1,2,0:T(8,128)S(1)}, ...), condition=%wide.region_8.9_spmd, body=%wide.region_5.8_spmd.sunk | while | flops 1389350400 | bytes 79177912 | solution.py:147
  164.0 8.8 %select_reduce_fusion.3 = (f32[16,512]{1,0:T(8,128)S(1)}, f32[16,512,512]{1,2,0:T(8,128)}) fusion(pred[512,512]{0,1:T(8,128)(4,1)S(1)} %and_or_fusion.2, bf16[512,16,80]{0,2,1:T(8,128)(2,1)S(1)} %bitcast.97, bf16[512,16,80]{0,2,1:T(8,128)(2,1)} %bitcast.99), kind=kOutput, calls=%fused_computation.1.clone.1 | convolution fusion | flops 683663360 | bytes 19693568 | tf_op jit(solution)/shard_map/while/body/eval_jaxpr/qhd,khd->hqk/dot_general | solution.py:60
  172.8 9.3 %fusion.54 = f32[16,512]{1,0:T(8,128)S(1)} fusion(f32[16,512,512]{1,2,0:T(8,128)} %get-tuple-element.323, f32[16,512]{1,0:T(8,128)S(1)} %get-tuple-element.324, pred[512,512]{0,1:T(8,128)(4,1)S(1)} %and_or_fusion.2), kind=kLoop, calls=%fused_computation.3.clone.1 | loop fusion | flops 16769024 | bytes 17104896 | tf_op jit(solution)/shard_map/while/body/eval_jaxpr/reduce_sum | solution.py:73
  182.1 9.1 %fusion.55 = f32[16,512,80]{1,2,0:T(8,128)} fusion(bf16[512,16,80]{0,2,1:T(8,128)(2,1)S(1)} %bitcast.111, f32[16,512,512]{1,2,0:T(8,128)} %get-tuple-element.323, f32[16,512]{1,0:T(8,128)S(1)} %get-tuple-element.324, pred[512,512]{0,1:T(8,128)(4,1)S(1)} %and_or_fusion.2), kind=kOutput, calls=%fused_computation.4.clone.1 | convolution fusion | flops 687865856 | bytes 21004288 | tf_op jit(solution)/shard_map/while/body/eval_jaxpr/hqk,khd->qhd/dot_general | solution.py:74
  191.2 2.1 copy.221
  199.5 8.8 %select_reduce_fusion.3 = (f32[16,512]{1,0:T(8,128)S(1)}, f32[16,512,512]{1,2,0:T(8,128)}) fusion(pred[512,512]{0,1:T(8,128)(4,1)S(1)} %and_or_fusion.2, bf16[512,16,80]{0,2,1:T(8,128)(2,1)S(1)} %bitcast.97, bf16[512,16,80]{0,2,1:T(8,128)(2,1)} %bitcast.99), kind=kOutput, calls=%fused_computation.1.clone.1 | convolution fusion | flops 683663360 | bytes 19693568 | tf_op jit(solution)/shard_map/while/body/eval_jaxpr/qhd,khd->hqk/dot_general | solution.py:60
  208.3 9.3 %fusion.54 = f32[16,512]{1,0:T(8,128)S(1)} fusion(f32[16,512,512]{1,2,0:T(8,128)} %get-tuple-element.323, f32[16,512]{1,0:T(8,128)S(1)} %get-tuple-element.324, pred[512,512]{0,1:T(8,128)(4,1)S(1)} %and_or_fusion.2), kind=kLoop, calls=%fused_computation.3.clone.1 | loop fusion | flops 16769024 | bytes 17104896 | tf_op jit(solution)/shard_map/while/body/eval_jaxpr/reduce_sum | solution.py:73
  217.6 9.1 %fusion.55 = f32[16,512,80]{1,2,0:T(8,128)} fusion(bf16[512,16,80]{0,2,1:T(8,128)(2,1)S(1)} %bitcast.111, f32[16,512,512]{1,2,0:T(8,128)} %get-tuple-element.323, f32[16,512]{1,0:T(8,128)S(1)} %get-tuple-element.324, pred[512,512]{0,1:T(8,128)(4,1)S(1)} %and_or_fusion.2), kind=kOutput, calls=%fused_computation.4.clone.1 | convolution fusion | flops 687865856 | bytes 21004288 | tf_op jit(solution)/shard_map/while/body/eval_jaxpr/hqk,khd->qhd/dot_general | solution.py:74
  226.7 2.1 copy.221
  234.2 3.5 all-to-all-start.1
  240.8 3.8 all-to-all-done.1
  244.6 3.3 all-to-all-start.2
  247.9 10.2 %copy.167 = f32[1,1024,1280]{2,0,1:T(1,128)} copy(f32[1,1024,1280]{2,1,0:T(8,128)} %bitcast.103) | data formatting | bytes 10485760 | tf_op jit(solution)/shard_map/broadcast_in_dim;reshape | solution.py:156
  258.1 6.3 %all-to-all-start = ((f32[1,1024,1280]{2,0,1:T(1,128)}), f32[1,1024,1280]{2,0,1:T(1,128)}, u32[]{:S(2)}, u32[]{:S(2)}) async-start(f32[1,1024,1280]{2,0,1:T(1,128)} %copy.167), calls=%async_computation.3 | async-start | bytes 10485760 | tf_op jit(solution)/shard_map/all_to_all | solution.py:156
  279.3 2.6 broadcast_in_dim.99
  281.9 5.9 %copy.173 = f32[8,128,1280]{2,1,0:T(8,128)} copy(f32[8,128,1280]{1,2,0:T(8,128)} %bitcast.102) | data formatting | bytes 10485760 | tf_op jit(solution)/shard_map/reshape | solution.py:161
  287.8 83.8 %all-to-all-done = f32[1,1024,1280]{2,0,1:T(1,128)} async-done(((f32[1,1024,1280]{2,0,1:T(1,128)}), f32[1,1024,1280]{2,0,1:T(1,128)}, u32[]{:S(2)}, u32[]{:S(2)}) %all-to-all-start) | async-done | bytes 5242912 | tf_op jit(solution)/shard_map/all_to_all | solution.py:156
  371.6 3.0 copy.202
  (160 shorter events, 69.8 us)
Async XLA Ops:
  6.5 1.0 copy-start
  6.5 38.2 %reduce-scatter.6.cloned.1.call-start = ((), (), s32[]{:S(2)}) async-start(), calls=%async_computation.7 | async-start | bytes 1966080 | tf_op jit(solution)/shard_map/reduce_scatter | solution.py:113
  19.6 50.7 %reduce-scatter.4.cloned.1.call-start = ((), (), s32[]{:S(2)}) async-start(), calls=%async_computation.6 | async-start | bytes 1966080 | tf_op jit(solution)/shard_map/reduce_scatter | solution.py:112
  24.6 89.4 %reduce-scatter.8.cloned.1.call-start = ((), (), s32[]{:S(2)}) async-start(), calls=%async_computation.8 | async-start | bytes 1966080 | tf_op jit(solution)/shard_map/reduce_scatter | solution.py:114
  75.3 65.4 %copy-start.3 = (bf16[128,1280]{1,0:T(8,128)(2,1)}, bf16[128,1280]{1,0:T(8,128)(2,1)S(1)}, u32[]{:S(2)}) copy-start(bf16[128,1280]{1,0:T(8,128)(2,1)S(1)} %get-tuple-element.237) | copy-start | bytes 983044
  75.3 12.0 %collective-permute-start = (bf16[128,1280]{1,0:T(8,128)(2,1)S(1)}, bf16[128,1280]{1,0:T(8,128)(2,1)S(1)}, u32[]{:S(2)}, u32[]{:S(2)}) collective-permute-start(bf16[128,1280]{1,0:T(8,128)(2,1)S(1)} %get-tuple-element.236), channel_id=1, source_target_pairs={{0,2},{2,4},{4,6},{6,8},{8,10},{10,12},{12,14},{14,0},{1,3},{3,5},... | collective-permute-start | bytes 983048 | tf_op jit(solution)/shard_map/ppermute | solution.py:20
  87.4 21.4 %copy-start.6 = (bf16[128,1280]{1,0:T(8,128)(2,1)}, bf16[128,1280]{1,0:T(8,128)(2,1)S(1)}, u32[]{:S(2)}) copy-start(bf16[128,1280]{1,0:T(8,128)(2,1)S(1)} %collective-permute-done) | copy-start | bytes 983044
  87.4 11.1 %collective-permute-start.1 = (bf16[128,1280]{1,0:T(8,128)(2,1)S(1)}, bf16[128,1280]{1,0:T(8,128)(2,1)S(1)}, u32[]{:S(2)}, u32[]{:S(2)}) collective-permute-start(bf16[128,1280]{1,0:T(8,128)(2,1)S(1)} %collective-permute-done), channel_id=1, source_target_pairs={{0,2},{2,4},{4,6},{6,8},{8,10},{10,12},{12,14},{14,0},{1,3},{3,5},... | collective-permute-start | bytes 983048 | tf_op jit(solution)/shard_map/ppermute | solution.py:20
  98.5 10.3 %copy-start.8 = (bf16[128,1280]{1,0:T(8,128)(2,1)}, bf16[128,1280]{1,0:T(8,128)(2,1)S(1)}, u32[]{:S(2)}) copy-start(bf16[128,1280]{1,0:T(8,128)(2,1)S(1)} %collective-permute-done.1) | copy-start | bytes 983044
  98.5 10.3 %collective-permute-start.2 = (bf16[128,1280]{1,0:T(8,128)(2,1)S(1)}, bf16[128,1280]{1,0:T(8,128)(2,1)S(1)}, u32[]{:S(2)}, u32[]{:S(2)}) collective-permute-start(bf16[128,1280]{1,0:T(8,128)(2,1)S(1)} %collective-permute-done.1), channel_id=1, source_target_pairs={{0,2},{2,4},{4,6},{6,8},{8,10},{10,12},{12,14},{14,0},{1,3},{3,5},... | collective-permute-start | bytes 983048 | tf_op jit(solution)/shard_map/ppermute | solution.py:20
  108.7 9.9 %copy-start.10 = (bf16[128,1280]{1,0:T(8,128)(2,1)}, bf16[128,1280]{1,0:T(8,128)(2,1)S(1)}, u32[]{:S(2)}) copy-start(bf16[128,1280]{1,0:T(8,128)(2,1)S(1)} %collective-permute-done.2) | copy-start | bytes 983044
  108.7 9.9 %collective-permute-start.3 = (bf16[128,1280]{1,0:T(8,128)(2,1)S(1)}, bf16[128,1280]{1,0:T(8,128)(2,1)}, u32[]{:S(2)}, u32[]{:S(2)}) collective-permute-start(bf16[128,1280]{1,0:T(8,128)(2,1)S(1)} %collective-permute-done.2), channel_id=1, source_target_pairs={{0,2},{2,4},{4,6},{6,8},{8,10},{10,12},{12,14},{14,0},{1,3},{3,5},... | collective-permute-start | bytes 983048 | tf_op jit(solution)/shard_map/ppermute | solution.py:20
  108.8 9.9 %collective-permute-start.7 = (bf16[128,1280]{1,0:T(8,128)(2,1)S(1)}, bf16[128,1280]{1,0:T(8,128)(2,1)}, u32[]{:S(2)}, u32[]{:S(2)}) collective-permute-start(bf16[128,1280]{1,0:T(8,128)(2,1)S(1)} %get-tuple-element.237), channel_id=1, source_target_pairs={{0,16},{1,17},{2,18},{3,19},{4,20},{5,21},{6,22},{7,23},{8,24},{9,... | collective-permute-start | bytes 983048 | tf_op jit(solution)/shard_map/ppermute | solution.py:33
  115.9 12.8 %collective-permute-start.8 = (bf16[128,1280]{1,0:T(8,128)(2,1)}, bf16[128,1280]{1,0:T(8,128)(2,1)}, u32[]{:S(2)}, u32[]{:S(2)}) collective-permute-start(bf16[128,1280]{1,0:T(8,128)(2,1)} %convert_element_type.57), channel_id=1, source_target_pairs={{0,16},{1,17},{2,18},{3,19},{4,20},{5,21},{6,22},{7,23},{8,24},{9,... | collective-permute-start | bytes 983048 | tf_op jit(solution)/shard_map/ppermute | solution.py:33
  118.6 10.1 %collective-permute-start.4 = (bf16[128,1280]{1,0:T(8,128)(2,1)}, bf16[128,1280]{1,0:T(8,128)(2,1)}, u32[]{:S(2)}, u32[]{:S(2)}) collective-permute-start(bf16[128,1280]{1,0:T(8,128)(2,1)} %collective-permute-done.3), channel_id=1, source_target_pairs={{0,2},{2,4},{4,6},{6,8},{8,10},{10,12},{12,14},{14,0},{1,3},{3,5},... | collective-permute-start | bytes 983048 | tf_op jit(solution)/shard_map/ppermute | solution.py:20
  128.7 10.4 %collective-permute-start.5 = (bf16[128,1280]{1,0:T(8,128)(2,1)}, bf16[128,1280]{1,0:T(8,128)(2,1)}, u32[]{:S(2)}, u32[]{:S(2)}) collective-permute-start(bf16[128,1280]{1,0:T(8,128)(2,1)} %collective-permute-done.4), channel_id=1, source_target_pairs={{0,2},{2,4},{4,6},{6,8},{8,10},{10,12},{12,14},{14,0},{1,3},{3,5},... | collective-permute-start | bytes 983048 | tf_op jit(solution)/shard_map/ppermute | solution.py:20
  130.6 23.1 %copy-start.7 = (bf16[128,1280]{1,0:T(8,128)(2,1)S(1)}, bf16[128,1280]{1,0:T(8,128)(2,1)}, u32[]{:S(2)}) copy-start(bf16[128,1280]{1,0:T(8,128)(2,1)} %copy-done.6) | copy-start | bytes 983044
  139.1 10.5 %collective-permute-start.6 = (bf16[128,1280]{1,0:T(8,128)(2,1)}, bf16[128,1280]{1,0:T(8,128)(2,1)}, u32[]{:S(2)}, u32[]{:S(2)}) collective-permute-start(bf16[128,1280]{1,0:T(8,128)(2,1)} %collective-permute-done.5), channel_id=1, source_target_pairs={{0,2},{2,4},{4,6},{6,8},{8,10},{10,12},{12,14},{14,0},{1,3},{3,5},... | collective-permute-start | bytes 983048 | tf_op jit(solution)/shard_map/ppermute | solution.py:20
  140.8 12.9 %copy-start.11 = (bf16[128,1280]{1,0:T(8,128)(2,1)S(1)}, bf16[128,1280]{1,0:T(8,128)(2,1)}, u32[]{:S(2)}) copy-start(bf16[128,1280]{1,0:T(8,128)(2,1)} %copy-done.10) | copy-start | bytes 983044
  140.8 12.9 %copy-start.9 = (bf16[128,1280]{1,0:T(8,128)(2,1)S(1)}, bf16[128,1280]{1,0:T(8,128)(2,1)}, u32[]{:S(2)}) copy-start(bf16[128,1280]{1,0:T(8,128)(2,1)} %copy-done.8) | copy-start | bytes 983044
  172.8 9.3 %copy-start.5 = (bf16[512,1280]{0,1:T(8,128)(2,1)S(1)}, bf16[512,1280]{0,1:T(8,128)(2,1)}, u32[]{:S(2)}) copy-start(bf16[512,1280]{0,1:T(8,128)(2,1)} %get-tuple-element.361) | copy-start | bytes 3932164 | tf_op jit(solution)/shard_map/while
  208.3 9.3 %copy-start.5 = (bf16[512,1280]{0,1:T(8,128)(2,1)S(1)}, bf16[512,1280]{0,1:T(8,128)(2,1)}, u32[]{:S(2)}) copy-start(bf16[512,1280]{0,1:T(8,128)(2,1)} %get-tuple-element.361) | copy-start | bytes 3932164 | tf_op jit(solution)/shard_map/while
  234.2 10.4 %all-to-all-start.1 = ((f32[8,1,2048]{2,1,0:T(1,128)}), f32[8,1,2048]{2,1,0:T(1,128)S(1)}, u32[]{:S(2)}, u32[]{:S(2)}) async-start(f32[8,1,2048]{2,1,0:T(1,128)} %reshape.390), calls=%async_computation.4 | async-start | bytes 131072 | tf_op jit(solution)/shard_map/all_to_all | solution.py:154
  244.6 13.5 %all-to-all-start.2 = ((f32[8,1,2048]{2,1,0:T(1,128)}), f32[8,1,2048]{2,1,0:T(1,128)S(1)}, u32[]{:S(2)}, u32[]{:S(2)}) async-start(f32[8,1,2048]{2,1,0:T(1,128)} %reshape.392), calls=%async_computation.5 | async-start | bytes 131072 | tf_op jit(solution)/shard_map/all_to_all | solution.py:155
  258.1 6.4 %copy-start.4 = (bf16[128,1280]{1,0:T(8,128)(2,1)S(1)}, bf16[128,1280]{1,0:T(8,128)(2,1)}, u32[]{:S(2)}) copy-start(bf16[128,1280]{1,0:T(8,128)(2,1)} %copy-done.3) | copy-start | bytes 983044
  258.1 113.5 %all-to-all-start = ((f32[1,1024,1280]{2,0,1:T(1,128)}), f32[1,1024,1280]{2,0,1:T(1,128)}, u32[]{:S(2)}, u32[]{:S(2)}) async-start(f32[1,1024,1280]{2,0,1:T(1,128)} %copy.167), calls=%async_computation.3 | async-start | bytes 10485760 | tf_op jit(solution)/shard_map/all_to_all | solution.py:156
  371.6 4.0 %copy-start.2 = (f32[8,128,1280]{2,1,0:T(8,128)S(1)}, f32[8,128,1280]{2,1,0:T(8,128)}, u32[]{:S(2)}) copy-start(f32[8,128,1280]{2,1,0:T(8,128)} %copy.173) | copy-start | bytes 15728644
  374.5 2.9 copy-start.1
Sparse Core Ops, SparseCore 0:
  19.7 25.0 reduce-scatter.5
  47.0 23.2 reduce-scatter.3
  72.6 23.2 reduce-scatter.7
